TPU v7x, 256 devices: a whole 4x4x8 slice. The times are simulated.
256 devices in a mesh: dp: 4 (over z_hi), row: 16 (over y, x), col: 4 (over z_lo, core).
Axes of the slice: x: 4, y: 4, z: 8 (z_hi: 4, z_lo: 2; z = z_hi * 2 + z_lo), core: 2. Of those that a mesh axis runs over, the one named last changes fastest.
Arguments:
- grad_partials: float32 [4, 4, 2048, 16384], P('dp', None, 'row', 'col'), may hold values from -300 to 300, as said below
- master_weights: float32 [8192, 16384], P(('dp', 'row'), 'col'), may hold values from -1.5 to 1.5
- row_moment: float32 [8192], P(('dp', 'row')), may hold values from 0.3 to 30
- col_moment: float32 [16384], P('col'), may hold values from 0.003 to 0.3
Outputs:
- new_master: float32 [8192, 16384], P(('dp', 'row'), 'col')
- new_row_moment: float32 [8192], P(('dp', 'row'))
- new_col_moment: float32 [16384], P('col')
- compute_weights: bfloat16 [4, 2048, 16384], P(None, 'row', 'col')
- rms_update: float32 [], replicated
Inputs may be any that keep to these rules, and one draw needn't show every extreme that they name: `grad_partials`: finite gradient partials.
All inputs are finite; a program needn't handle non-finite values.
Results may differ from a plain program's by a relative error of at most 0.0004.
Values may be sent and summed in bfloat16 or wider, within the bound.
A program may use at most 128 MiB of HBM per device.

v0:
```python
import jax
import jax.numpy as jnp
from jax import lax
from jax.sharding import PartitionSpec as P

decay_rate = 0.9
step_rate = 0.05
tiny_value = 1e-30


def local(grad_partials, master_weights, row_moment, col_moment):
    local_grads = grad_partials[0]
    row_dev = master_weights.shape[0]
    col_dev = master_weights.shape[1]
    groups = lax.axis_size("dp")
    all_rows = row_dev * groups * lax.axis_size("row")
    full_width = col_dev * lax.axis_size("col")
    summed = lax.psum_scatter(local_grads, "dp", scatter_dimension=0, tiled=True)
    gradient = summed.reshape(row_dev, col_dev)
    weights_all, moments_all = (master_weights, row_moment)
    squared = gradient * gradient
    row_totals = lax.psum(jnp.sum(squared, axis=1), "col")
    local_cols = jnp.sum(squared, axis=0)
    row_mean = row_totals / full_width + tiny_value
    new_rows = decay_rate * moments_all + (1.0 - decay_rate) * row_mean
    rows_sum = jnp.sum(new_rows)
    col_totals, moment_sum = lax.psum((local_cols, rows_sum), ("dp", "row"))
    col_mean = col_totals / all_rows + tiny_value
    new_cols = decay_rate * col_moment + (1.0 - decay_rate) * col_mean
    scale_mean = moment_sum / all_rows
    update = gradient * lax.rsqrt(new_rows[:, None] * new_cols[None, :] / scale_mean)
    update_local = jnp.sum(update * update)
    update_sum = lax.psum(update_local, ("dp", "row", "col"))
    entry_count = float(all_rows * full_width)
    rms_update = jnp.sqrt(update_sum / entry_count)
    new_weights = weights_all - step_rate * update / jnp.maximum(1.0, rms_update)
    copies = lax.all_gather(new_weights.astype(jnp.bfloat16)[None], "dp", axis=0, tiled=True)
    return (new_weights, new_rows, new_cols, copies, rms_update)


def solution(mesh):
    return jax.shard_map(
        local,
        mesh=mesh,
        in_specs=(P("dp", None, "row", "col"), P(("dp", "row"), "col"), P(("dp", "row")), P("col")),
        out_specs=(P(("dp", "row"), "col"), P(("dp", "row")), P("col"), P(None, "row", "col"), P()),
        check_vma=False,
    )
```

profile of v0, /device:TPU:37, one launch (start us, length us, event | category | flops | bytes accessed | tf_op | source)
XLA Modules:
  0.0 726.3 jit_solution(2824089146126804063)
XLA Ops:
  7.2 0.0 reduce-scatter.2.cloned.1.call-start
  7.2 0.7 reduce-scatter.2.cloned.1.call-update
  7.9 0.0 copy-start.4
  7.9 0.0 copy-start.2
  7.9 0.0 all-gather.3.cloned.1.call-start
  8.0 155.5 %reduce-scatter.2.cloned.1.call-done = f32[1,128,4096]{2,1,0:T(8,128)} async-done(((f32[4,128,4096]{2,1,0:T(8,128)}), f32[1,128,4096]{2,1,0:T(8,128)}) %reduce-scatter.2.cloned.1.call-update) | async-done | bytes 2097168 | tf_op jit(solution)/shard_map/reduce_scatter | solution.py:18
  163.5 0.0 copy-start
  163.5 2.0 fusion
  165.5 9.4 %psum.28 = f32[128]{0:T(128)S(1)} all-reduce(f32[128]{0:T(128)S(1)} %get-tuple-element.6), channel_id=1, replica_groups=mesh['dp'=4,'row'=16,'col'=4] {'col'}, use_global_device_ids=true, to_apply=%region_2.0 | all-reduce | flops 128 | bytes 1024 | tf_op jit(solution)/shard_map/psum | solution.py:22
  174.9 0.0 copy-done.4
  174.9 0.6 fusion.3
  175.5 0.0 copy-start.3
  175.5 313.2 %all-reduce = (f32[]{:T(128)}, f32[4096]{0:T(1024)S(1)}) all-reduce(f32[]{:T(128)} %get-tuple-element.11, f32[4096]{0:T(1024)S(1)} %get-tuple-element.5), channel_id=1, replica_groups=mesh['dp'=4,'row'=16,'col'=4] {'dp','row'}, use_global_device_ids=true, to_apply=%region_6.0 | all-reduce | flops 4097 | bytes 32776 | tf_op jit(solution)/shard_map/psum | solution.py:27
  489.4 0.0 copy-done.2
  489.4 0.0 copy-start.1
  489.4 0.0 copy-done
  489.4 1.2 multiply_reduce_fusion
  490.6 134.0 %psum.31 = f32[]{:T(128)} all-reduce(f32[]{:T(128)} %multiply_reduce_fusion), channel_id=1, replica_groups=mesh['dp'=4,'row'=16,'col'=4] {'dp','row','col'}, use_global_device_ids=true, to_apply=%region_8.0 | all-reduce | flops 1 | bytes 8 | tf_op jit(solution)/shard_map/psum | solution.py:33
  625.4 3.9 fusion.2
  629.3 0.0 copy-done.3
  629.3 0.0 copy-done.1
  629.3 0.0 all-gather.3.cloned.1.call-update
  629.3 84.4 %all-gather.3.cloned.1.call-done = bf16[512,4096]{1,0:T(8,128)(2,1)} async-done(((bf16[128,4096]{1,0:T(8,128)(2,1)}), bf16[512,4096]{1,0:T(8,128)(2,1)}) %all-gather.3.cloned.1.call-update) | async-done | bytes 4194320 | tf_op jit(solution)/shard_map/all_gather | solution.py:37
  713.6 4.7 copy.10
  (1 shorter events, 0.0 us)
Async XLA Ops:
  7.2 156.3 %reduce-scatter.2.cloned.1.call-start = ((), (), s32[]{:S(2)}) async-start(), calls=%async_computation.1 | async-start | bytes 10485760 | tf_op jit(solution)/shard_map/reduce_scatter | solution.py:18
  7.9 167.0 %copy-start.4 = (f32[128]{0:T(128)S(1)}, f32[128]{0:T(128)}, u32[]{:S(2)}) copy-start(f32[128]{0:T(128)} %param.6) | copy-start | bytes 1540
  7.9 481.4 %copy-start.2 = (f32[4096]{0:T(1024)S(1)}, f32[4096]{0:T(1024)}, u32[]{:S(2)}) copy-start(f32[4096]{0:T(1024)} %param.7) | copy-start | bytes 49156
  7.9 705.7 %all-gather.3.cloned.1.call-start = ((), (), s32[]{:S(2)}) async-start(), calls=%async_computation.2 | async-start | bytes 5242880 | tf_op jit(solution)/shard_map/all_gather | solution.py:37
  163.5 325.9 %copy-start = (f32[1,128,4096]{2,1,0:T(8,128)S(1)}, f32[1,128,4096]{2,1,0:T(8,128)}, u32[]{:S(2)}) copy-start(f32[1,128,4096]{2,1,0:T(8,128)} %reduce-scatter.2.cloned.1.call-done) | copy-start | bytes 6291460
  175.5 453.8 %copy-start.3 = (f32[128]{0:T(128)}, f32[128]{0:T(128)S(1)}, u32[]{:S(2)}) copy-start(f32[128]{0:T(128)S(1)} %get-tuple-element.19) | copy-start | bytes 1540
  489.4 139.9 %copy-start.1 = (f32[4096]{0:T(1024)}, f32[4096]{0:T(1024)S(1)}, u32[]{:S(2)}) copy-start(f32[4096]{0:T(1024)S(1)} %multiply_add_fusion) | copy-start | bytes 49156
Sparse Core Ops, SparseCore 0:
  10.6 152.8 reduce-scatter.1
  629.4 84.1 all-gather.2
where the time goes:
time: 727 us; the launch traced here: 726 us
  blocking collectives  457 us (63%)
  waiting for transfers between devices  241 us (33%)
  between operations  16.6 us (2%)
  other arithmetic  7.76 us (1%)
    psum x1, blocking collectives, local(): col_totals, moment_sum = lax.psum((local_cols, rows_sum), ('dp', 'row'))  313 us
    reduce_scatter x1, waiting for transfers between devices, local(): lax.psum_scatter(local_grads, 'dp', scatter_dimension=0, tiled=True)  155 us
    psum x1, blocking collectives, local(): update_sum = lax.psum(update_local, ('dp', 'row', 'col'))  134 us
    all_gather x1, waiting for transfers between devices, local(): lax.all_gather(new_weights.astype(jnp.bfloat16)[None], 'dp', axis=0, tile...  84.4 us
  transfers between devices with their start and end apart: 2, of which 2 were waited for; matrix products, arithmetic and copies ran while one was open for 0% of the time, Pallas kernels for 0%

commit v1 on v0

--- a/solution.py
+++ b/solution.py
@@ -34,7 +34,9 @@
     entry_count = float(all_rows * full_width)
     rms_update = jnp.sqrt(update_sum / entry_count)
     new_weights = weights_all - step_rate * update / jnp.maximum(1.0, rms_update)
-    copies = lax.all_gather(new_weights.astype(jnp.bfloat16)[None], "dp", axis=0, tiled=True)
+    block = new_weights.astype(jnp.bfloat16)[None]
+    sent = jnp.stack([block] * lax.axis_size("dp"))
+    copies = jnp.concatenate(lax.all_to_all(sent, "dp", 0, 0), axis=0)
     return (new_weights, new_rows, new_cols, copies, rms_update)
 
 

time: 727 us -> 740 us (1.018)
  blocking collectives: 457 us -> 554 us
  waiting for transfers between devices: 241 us -> 156 us
    all_to_all x0 -> x1, blocking collectives: none -> 97.9 us  [local(): copies = jnp.concatenate(lax.all_to_all(sent, 'dp', 0, 0), axis=0)]
    all_gather x1 -> x0, waiting for transfers between devices: 84.4 us -> none  [local(): lax.all_gather(new_weights.astype(jnp.bfloat16)[None], 'dp', axis=0, tile...]
  transfers between devices with their start and end apart: 2 -> 1, of which waited for: 2 -> 1; matrix products, arithmetic and copies ran while one was open for 0% -> 0% of each run, Pallas kernels for 0% -> 0%
where the time goes in v1:
time: 740 us; the launch traced here: 737 us
  blocking collectives  554 us (75%)
  waiting for transfers between devices  156 us (21%)
  between operations  16.6 us (2%)
  other arithmetic  7.42 us (1%)
    psum x1, blocking collectives, local(): col_totals, moment_sum = lax.psum((local_cols, rows_sum), ('dp', 'row'))  313 us
    reduce_scatter x1, waiting for transfers between devices, local(): lax.psum_scatter(local_grads, 'dp', scatter_dimension=0, tiled=True)  156 us
    psum x1, blocking collectives, local(): update_sum = lax.psum(update_local, ('dp', 'row', 'col'))  134 us
    all_to_all x1, blocking collectives, local(): copies = jnp.concatenate(lax.all_to_all(sent, 'dp', 0, 0), axis=0)  97.9 us
  transfers between devices with their start and end apart: 1, of which 1 were waited for; matrix products, arithmetic and copies ran while one was open for 0% of the time, Pallas kernels for 0%

profile of v1, /device:TPU:37, one launch (start us, length us, event | category | flops | bytes accessed | tf_op | source)
XLA Modules:
  0.0 737.3 jit_solution(15551591234515425267)
XLA Ops:
  7.2 0.0 reduce-scatter.2.cloned.1.call-start
  7.2 0.7 reduce-scatter.2.cloned.1.call-update
  7.9 0.0 copy-start.4
  7.9 0.0 copy-start.2
  7.9 155.5 %reduce-scatter.2.cloned.1.call-done = f32[1,128,4096]{2,1,0:T(8,128)} async-done(((f32[4,128,4096]{2,1,0:T(8,128)}), f32[1,128,4096]{2,1,0:T(8,128)}) %reduce-scatter.2.cloned.1.call-update) | async-done | bytes 2097168 | tf_op jit(solution)/shard_map/reduce_scatter | solution.py:18
  163.5 0.0 copy-start
  163.5 2.0 fusion
  165.5 9.4 %psum.28 = f32[128]{0:T(128)S(1)} all-reduce(f32[128]{0:T(128)S(1)} %get-tuple-element.6), channel_id=1, replica_groups=mesh['dp'=4,'row'=16,'col'=4] {'col'}, use_global_device_ids=true, to_apply=%region_2.0 | all-reduce | flops 128 | bytes 1024 | tf_op jit(solution)/shard_map/psum | solution.py:22
  174.9 0.0 copy-done.4
  174.9 0.6 fusion.3
  175.5 0.0 copy-start.3
  175.5 313.2 %all-reduce = (f32[]{:T(128)}, f32[4096]{0:T(1024)S(1)}) all-reduce(f32[]{:T(128)} %get-tuple-element.11, f32[4096]{0:T(1024)S(1)} %get-tuple-element.5), channel_id=1, replica_groups=mesh['dp'=4,'row'=16,'col'=4] {'dp','row'}, use_global_device_ids=true, to_apply=%region_6.0 | all-reduce | flops 4097 | bytes 32776 | tf_op jit(solution)/shard_map/psum | solution.py:27
  489.4 0.0 copy-done.2
  489.4 0.0 copy-start.1
  489.4 0.0 copy-done
  489.4 1.2 multiply_reduce_fusion
  490.6 134.0 %psum.31 = f32[]{:T(128)} all-reduce(f32[]{:T(128)} %multiply_reduce_fusion), channel_id=1, replica_groups=mesh['dp'=4,'row'=16,'col'=4] {'dp','row','col'}, use_global_device_ids=true, to_apply=%region_8.0 | all-reduce | flops 1 | bytes 8 | tf_op jit(solution)/shard_map/psum | solution.py:33
  625.4 3.5 fusion.2
  628.9 0.0 copy-done.3
  628.9 0.0 copy-done.1
  628.9 0.5 stack.3
  629.4 97.9 %all_to_all.5 = bf16[4,1,128,4096]{3,2,1,0:T(8,128)(2,1)S(1)} all-to-all(bf16[4,1,128,4096]{3,2,1,0:T(8,128)(2,1)S(1)} %stack.3), channel_id=1, replica_groups=mesh['dp'=4,'row'=16,'col'=4] {'dp'}, dimensions={0} | all-to-all | bytes 8388608 | tf_op jit(solution)/shard_map/all_to_all | solution.py:39
  727.3 2.0 copy.10
  (1 shorter events, 0.0 us)
Async XLA Ops:
  7.2 156.3 %reduce-scatter.2.cloned.1.call-start = ((), (), s32[]{:S(2)}) async-start(), calls=%async_computation.2 | async-start | bytes 10485760 | tf_op jit(solution)/shard_map/reduce_scatter | solution.py:18
  7.9 167.0 %copy-start.4 = (f32[128]{0:T(128)S(1)}, f32[128]{0:T(128)}, u32[]{:S(2)}) copy-start(f32[128]{0:T(128)} %param.6) | copy-start | bytes 1540
  7.9 481.4 %copy-start.2 = (f32[4096]{0:T(1024)S(1)}, f32[4096]{0:T(1024)}, u32[]{:S(2)}) copy-start(f32[4096]{0:T(1024)} %param.7) | copy-start | bytes 49156
  163.5 325.9 %copy-start = (f32[1,128,4096]{2,1,0:T(8,128)S(1)}, f32[1,128,4096]{2,1,0:T(8,128)}, u32[]{:S(2)}) copy-start(f32[1,128,4096]{2,1,0:T(8,128)} %reduce-scatter.2.cloned.1.call-done) | copy-start | bytes 6291460
  175.5 453.4 %copy-start.3 = (f32[128]{0:T(128)}, f32[128]{0:T(128)S(1)}, u32[]{:S(2)}) copy-start(f32[128]{0:T(128)S(1)} %get-tuple-element.19) | copy-start | bytes 1540
  489.4 139.5 %copy-start.1 = (f32[4096]{0:T(1024)}, f32[4096]{0:T(1024)S(1)}, u32[]{:S(2)}) copy-start(f32[4096]{0:T(1024)S(1)} %multiply_add_fusion) | copy-start | bytes 49156
Sparse Core Ops, SparseCore 0:
  10.6 152.8 reduce-scatter.1
